TPU v7x, 32 devices: a whole 2x2x4 slice. The times are simulated.
32 devices in a mesh: grp: 2 (over x), tp: 8 (over z, y), rb: 2 (over core).
Axes of the slice: x: 2, y: 2, z: 4, core: 2. Of those that a mesh axis runs over, the one named last changes fastest.
Arguments:
- peram: bfloat16 [2048, 24, 2, 1024], P(('grp', 'tp'), None, None, 'rb'), parts along dimension 0, may hold values from -1 to 1
- src_elems: bfloat16 [14, 2, 256, 256], P('grp'), parts along dimension 0, may hold values from -0.25 to 0.25
- owner_times: int32 [16, 2], P('grp'), parts along dimension 0, may hold values from 0 to 23
- diag_mom: int32 [16, 2, 2], P(('grp', 'tp')), parts along dimension 0, may hold values from 0 to 6
- diag_count: int32 [16], P(('grp', 'tp')), parts along dimension 0, may hold values from 1 to 2, as said below
Outputs:
- corr: float32 [16, 2, 2, 2], P(('grp', 'tp')), parts along dimension 0
There are 2 independent parts, one for each index of `grp`. A program takes and returns all parts, laid end to end along the dimension named above; each array names one. Nothing has to cross between parts.
Inputs may be any that keep to these rules, and one draw needn't show every extreme that they name: `diag_count`: some pair has 2 assignments.
All inputs are finite; a program needn't handle non-finite values.
Results may differ from a plain program's by a relative error of at most 0.0031.
Values may be sent and summed in bfloat16 or wider, within the bound.
A program may use at most 128 MiB of HBM per device.

v0:
```python
import jax
import jax.numpy as jnp
from jax import lax
from jax.sharding import PartitionSpec as P


def paired_rhs(factor_part):
    swapped = jnp.stack([factor_part[:, 1], -factor_part[:, 0]], axis=1)
    return jnp.stack([factor_part, swapped], axis=0)


def contract_rows(left_rows, right_pair):
    return lax.dot_general(
        left_rows, right_pair, (((1, 2), (2, 3)), ((), ())), preferred_element_type=jnp.float32
    )


def trace_block(flipped, diag_block):
    block_f = diag_block.astype(jnp.float32)
    flip_f = flipped.astype(jnp.float32)
    real_sum = jnp.sum(flip_f[0] * block_f[:, 0] - flip_f[1] * block_f[:, 1])
    imag_sum = jnp.sum(flip_f[0] * block_f[:, 1] + flip_f[1] * block_f[:, 0])
    return (real_sum, imag_sum)


def shards(peram, src_elems, owner_times, diag_mom, diag_count):
    rb_count = lax.axis_size("rb")
    rb_rank = lax.axis_index("rb")
    picked = jnp.take(peram, owner_times, axis=1)
    arrived = lax.all_to_all(picked, "tp", split_axis=1, concat_axis=0, tiled=True)
    factor = arrived[:, 0]
    total_rows = factor.shape[0]
    row_count = total_rows // rb_count
    eig_count = src_elems.shape[-1]
    spin_total = total_rows // eig_count
    local_spins = row_count // eig_count
    diag_total = diag_mom.shape[1]
    right_pairs = [paired_rhs(factor[:, time_slot]) for time_slot in range(2)]
    summed = lax.psum_scatter(
        jnp.stack(
            [contract_rows(factor[:, time_slot], right_pairs[time_slot]) for time_slot in range(2)],
            axis=1,
        ),
        "rb",
        scatter_dimension=0,
        tiled=True,
    )
    meson_rows = summed.astype(jnp.bfloat16)
    meson_a = meson_rows[:, 0]
    meson_b = meson_rows[:, 1]
    owned = diag_count[0]
    results = []
    for slot_index in range(diag_total):
        elem_three = lax.dynamic_index_in_dim(
            src_elems, diag_mom[0, slot_index, 0], 0, keepdims=False
        )
        elem_four = lax.dynamic_index_in_dim(
            src_elems, diag_mom[0, slot_index, 1], 0, keepdims=False
        )
        flip_three = jnp.swapaxes(elem_three, 1, 2)
        flip_four = jnp.swapaxes(elem_four, 1, 2)
        right_four = jnp.stack(
            [
                jnp.stack([elem_four[0], elem_four[1]], axis=1),
                jnp.stack([-elem_four[1], elem_four[0]], axis=1),
            ],
            axis=0,
        )
        left_three = jnp.stack(
            [
                jnp.stack([flip_three[0], flip_three[1]], axis=-1),
                jnp.stack([flip_three[1], -flip_three[0]], axis=-1),
            ],
            axis=1,
        )
        mixed = jnp.concatenate(
            [
                lax.dot_general(
                    left_three,
                    meson_a[spin_local * eig_count : (spin_local + 1) * eig_count],
                    (((2, 3), (0, 1)), ((), ())),
                    preferred_element_type=jnp.float32,
                )
                for spin_local in range(local_spins)
            ],
            axis=0,
        )
        cross_re = jnp.zeros((), jnp.float32)
        cross_im = jnp.zeros((), jnp.float32)
        for spin_index in range(spin_total):
            col_block = meson_b[:, :, spin_index * eig_count : (spin_index + 1) * eig_count]
            product = lax.dot_general(
                col_block,
                right_four,
                (((1, 2), (0, 1)), ((), ())),
                preferred_element_type=jnp.float32,
            )
            partner = mixed[:, :, spin_index * eig_count : (spin_index + 1) * eig_count]
            cross_re = cross_re + jnp.sum(
                product[:, 0] * partner[:, 0] - product[:, 1] * partner[:, 1]
            )
            cross_im = cross_im + jnp.sum(
                product[:, 0] * partner[:, 1] + product[:, 1] * partner[:, 0]
            )
        three_re = jnp.zeros((), jnp.float32)
        three_im = jnp.zeros((), jnp.float32)
        four_re = jnp.zeros((), jnp.float32)
        four_im = jnp.zeros((), jnp.float32)
        for spin_local in range(local_spins):
            global_spin = rb_rank * local_spins + spin_local
            block_a = lax.dynamic_slice_in_dim(
                meson_a[spin_local * eig_count : (spin_local + 1) * eig_count],
                global_spin * eig_count,
                eig_count,
                2,
            )
            block_b = lax.dynamic_slice_in_dim(
                meson_b[spin_local * eig_count : (spin_local + 1) * eig_count],
                global_spin * eig_count,
                eig_count,
                2,
            )
            add_re, add_im = trace_block(flip_three, block_a)
            three_re = three_re + add_re
            three_im = three_im + add_im
            add_re, add_im = trace_block(flip_four, block_b)
            four_re = four_re + add_re
            four_im = four_im + add_im
        values = jnp.stack([cross_re, cross_im, three_re, three_im, four_re, four_im])
        values = lax.psum(values, "rb")
        results.append(values)
    stacked = jnp.stack(results)
    direct_re = stacked[:, 2] * stacked[:, 4] - stacked[:, 3] * stacked[:, 5]
    direct_im = stacked[:, 2] * stacked[:, 5] + stacked[:, 3] * stacked[:, 4]
    direct = jnp.stack([direct_re, direct_im], axis=-1)
    crossed = stacked[:, 0:2]
    values_all = 0.25 * jnp.stack([direct, crossed], axis=1)
    keep = (jnp.arange(diag_total, dtype=jnp.int32) < owned)[:, None, None]
    return jnp.where(keep, values_all, jnp.zeros_like(values_all))[None]


def solution(mesh):
    in_specs = (
        P(("grp", "tp"), None, None, "rb"),
        P("grp", None, None, None),
        P("grp", None),
        P(("grp", "tp"), None, None),
        P(("grp", "tp")),
    )
    out_specs = P(("grp", "tp"), None, None, None)
    return jax.shard_map(shards, mesh=mesh, in_specs=in_specs, out_specs=out_specs, check_vma=False)
```

profile of v0, /device:TPU:0, one launch (start us, length us, event | category | flops | bytes accessed | tf_op | source)
XLA Modules:
  0.0 233.8 jit_solution(16534536423233338884)
XLA Ops:
  6.5 0.7 compare_select_fusion
  7.2 0.7 compare_and_fusion
  8.1 13.4 %gather_fusion = bf16[16,128,2,512]{3,2,1,0:T(2,128)(2,1)} fusion(bf16[128,24,2,512]{3,2,1,0:T(2,128)(2,1)} %param.5, s32[1024]{0:T(1024)S(1)} %pad_clamp_fusion), kind=kCustom, calls=%fused_computation | custom fusion | bytes 8388672 | tf_op jit(solution)/shard_map/jit(_take)/gather | solution.py:29
  21.5 5.1 %copy.38 = bf16[16,128,2,512]{3,1,2,0:T(8,128)(2,1)} copy(bf16[16,128,2,512]{3,2,1,0:T(2,128)(2,1)} %gather_fusion) | data formatting | bytes 8388608 | tf_op jit(solution)/shard_map/jit(_take)/gather | solution.py:29
  26.7 2.6 %select_bitcast_fusion = bf16[128,8,2,2,512]{4,0,3,2,1:T(8,128)(2,1)S(1)} fusion(bf16[8,2,128,2,512]{4,2,3,1,0:T(8,128)(2,1)} %bitcast.384, pred[8,2]{1,0:T(8,128)(4,1)S(1)} %copy.36), kind=kLoop, calls=%fused_computation.38 | loop fusion | flops 2097152 | bytes 8388624 | tf_op jit(solution)/shard_map/jit(_take)/select_n | solution.py:29
  29.3 100.3 %all_to_all.15 = bf16[128,8,2,2,512]{4,0,3,2,1:T(8,128)(2,1)S(1)} all-to-all(bf16[128,8,2,2,512]{4,0,3,2,1:T(8,128)(2,1)S(1)} %select_bitcast_fusion), channel_id=1, replica_groups=mesh['grp'=2,'tp'=8,'rb'=2] {'tp'}, dimensions={1} | all-to-all | bytes 8388608 | tf_op jit(solution)/shard_map/all_to_all | solution.py:30
  129.6 0.4 copy.39
  130.1 0.7 slice_bitcast_fusion.3
  130.8 0.3 fusion.52
  131.1 0.2 maximum_bitcast_fusion.1
  131.3 4.5 %fusion.8 = f32[1024,1,2,1024]{3,0,2,1:T(8,128)S(1)} fusion(bf16[1,1024,2,512]{3,1,2,0:T(8,128)(2,1)S(1)} %maximum_bitcast_fusion.1, bf16[1,1024,2,512]{3,1,2,0:T(8,128)(2,1)S(1)} %get-tuple-element.62, bf16[1024,2,2,512]{3,0,2,1:T(8,128)(2,1)S(1)} %bitcast.382), kind=kOutput, calls=%fused_computation.39 | convolution fusion | flops 4303355904 | bytes 14680064 | tf_op jit(solution)/shard_map/dot_general | solution.py:13
  135.8 0.2 maximum_bitcast_fusion
  136.0 4.5 %fusion.11 = f32[1024,1,2,1024]{3,0,2,1:T(8,128)S(1)} fusion(bf16[1,1024,2,512]{3,1,2,0:T(8,128)(2,1)S(1)} %maximum_bitcast_fusion, bf16[1,1024,2,512]{3,1,2,0:T(8,128)(2,1)S(1)} %get-tuple-element.61, bf16[1024,2,2,512]{3,0,2,1:T(8,128)(2,1)S(1)} %bitcast.383), kind=kOutput, calls=%fused_computation.40 | convolution fusion | flops 4303355904 | bytes 14680064 | tf_op jit(solution)/shard_map/dot_general | solution.py:13
  140.5 6.6 %pad_maximum_fusion = f32[1024,2,2,1024]{3,0,2,1:T(8,128)} fusion(f32[1024,1,2,1024]{3,0,2,1:T(8,128)S(1)} %fusion.8, f32[1024,1,2,1024]{3,0,2,1:T(8,128)S(1)} %fusion.11), kind=kLoop, calls=%fused_computation.1 | loop fusion | flops 4194304 | bytes 33554432 | tf_op jit(solution)/shard_map/stack | solution.py:40
  147.1 0.7 copy-done.8
  147.8 0.6 fusion.54
  157.2 0.8 maximum_bitcast_fusion.6
  158.1 0.8 maximum_bitcast_fusion.2
  159.0 1.1 bitcast_convert_fusion.4
  160.1 0.9 convert_bitcast_fusion
  161.1 10.4 %reduce-scatter.2.cloned.1.call-done = f32[512,2,2,1024]{3,0,2,1:T(8,128)} async-done(((f32[1024,2,2,1024]{3,0,2,1:T(8,128)}), f32[512,2,2,1024]{3,0,2,1:T(8,128)}) %reduce-scatter.2.cloned.1.call-update) | async-done | bytes 8388624 | tf_op jit(solution)/shard_map/reduce_scatter | solution.py:39
  171.5 4.0 %convert_element_type.59 = bf16[512,2,2,1024]{3,0,2,1:T(8,128)(2,1)S(1)} convert(f32[512,2,2,1024]{3,0,2,1:T(8,128)} %reduce-scatter.2.cloned.1.call-done) | non-fusion elementwise | flops 2097152 | bytes 12582912 | tf_op jit(solution)/shard_map/convert_element_type | solution.py:48
  175.6 0.2 slice_bitcast_fusion
  175.8 0.7 convolution_bitcast_fusion
  176.5 0.7 convolution_bitcast_fusion.1
  177.2 0.5 convolution_bitcast_fusion.5
  177.7 0.5 convolution_bitcast_fusion.6
  178.2 0.5 convolution_bitcast_fusion.4
  178.6 0.5 convolution_bitcast_fusion.7
  179.1 0.6 fusion.51
  179.7 0.7 convolution_bitcast_fusion.2
  180.4 2.1 convolution_bitcast_fusion.3
  182.5 1.5 convolution_bitcast_fusion.9
  184.0 1.5 convolution_bitcast_fusion.10
  185.4 1.5 convolution_bitcast_fusion.8
  186.9 1.5 convolution_bitcast_fusion.11
  188.4 0.8 bitcast_convert_fusion.2
  189.2 0.8 bitcast_convert_fusion
  190.1 0.8 bitcast_convert_fusion.3
  190.9 0.9 bitcast_convert_fusion.1
  191.8 1.1 add_reduce_fusion.1
  192.9 1.1 add_reduce_fusion
  198.9 2.5 %add_reduce_fusion.14 = (f32[]{:T(128)}, f32[]{:T(128)}, f32[]{:T(128)}, f32[]{:T(128)}, f32[]{:T(128)}, /*index=5*/f32[]{:T(128)}, f32[]{:T(128)}, f32[]{:T(128)}) fusion(f32[2,256,256]{2,1,0:T(8,128)} %get-tuple-element.106, f32[256,2,256]{2,0,1:T(8,128)} %bitcast_convert_fusion.2, f32[2,256,256]{2,1,0:T(8,128)} %get-tuple-element.105, ...), kind=kLoop, calls=%fused_computation.152 | loop fusion | flops 2097144 | bytes 2097184 | tf_op jit(solution)/shard_map/reduce_sum | solution.py:22
  204.0 2.2 add_reduce_fusion.12
  208.8 3.5 %add_reduce_fusion.5 = (f32[]{:T(128)}, f32[]{:T(128)}, f32[]{:T(128)}, f32[]{:T(128)}, f32[512,1,256]{2,0,1:T(8,128)S(1)}) fusion(f32[512,2,256]{2,0,1:T(8,128)} %convolution_bitcast_fusion.9, f32[256,2,1024]{2,0,1:T(8,128)S(1)} %convolution_bitcast_fusion.2, f32[256,2,1024]{2,0,1:T(8,128)} %convolution_bitcast_fusion.3, ...), kind=kLoop, calls=%fused_computation.105 | loop fusion | flops 3276796 | bytes 6815760 | tf_op jit(solution)/shard_map/reduce_sum | solution.py:102
  212.3 1.3 add_reduce_fusion.4
  223.7 2.5 %all-reduce = (f32[1,6]{1,0:T(1,128)S(1)}, f32[1,6]{1,0:T(1,128)S(1)}) all-reduce(f32[1,6]{1,0:T(1,128)S(1)} %bitcast.390, f32[1,6]{1,0:T(1,128)S(1)} %bitcast.391), channel_id=1, replica_groups=mesh['grp'=2,'tp'=8,'rb'=2] {'rb'}, use_global_device_ids=true, to_apply=%region_34.35 | all-reduce | flops 12 | bytes 96 | tf_op jit(solution)/shard_map/psum | solution.py:130
  226.4 0.6 copy.52
  (46 shorter events, 1.6 us)
Async XLA Ops:
  6.5 165.0 %reduce-scatter.2.cloned.1.call-start = ((), (), s32[]{:S(2)}) async-start(), calls=%async_computation.2 | async-start | bytes 25165824 | tf_op jit(solution)/shard_map/reduce_scatter | solution.py:39
  147.1 0.7 copy-start.8
  147.1 8.7 %copy-start.4 = (bf16[7,2,256,256]{3,2,1,0:T(8,128)(2,1)S(1)}, bf16[7,2,256,256]{3,2,1,0:T(8,128)(2,1)}, u32[]{:S(2)}) copy-start(bf16[7,2,256,256]{3,2,1,0:T(8,128)(2,1)} %param.6) | copy-start | bytes 5505028
  175.7 1.5 copy-start.5
  179.7 2.8 %copy-start.6 = (bf16[1,256,2,256]{1,3,2,0:T(8,128)(2,1)S(1)}, bf16[1,256,2,256]{1,3,2,0:T(8,128)(2,1)}, u32[]{:S(2)}) copy-start(bf16[1,256,2,256]{1,3,2,0:T(8,128)(2,1)} %get-tuple-element.89) | copy-start | bytes 786436
  179.7 2.8 %copy-start.7 = (bf16[1,256,2,256]{1,3,2,0:T(8,128)(2,1)S(1)}, bf16[1,256,2,256]{1,3,2,0:T(8,128)(2,1)}, u32[]{:S(2)}) copy-start(bf16[1,256,2,256]{1,3,2,0:T(8,128)(2,1)} %get-tuple-element.90) | copy-start | bytes 786436
  192.9 11.1 %copy-start.1 = (f32[2,256,256]{2,1,0:T(8,128)S(1)}, f32[2,256,256]{2,1,0:T(8,128)}, u32[]{:S(2)}) copy-start(f32[2,256,256]{2,1,0:T(8,128)} %get-tuple-element.108) | copy-start | bytes 1572868
  206.2 6.1 %copy-start.2 = (f32[512,2,256]{2,0,1:T(8,128)S(1)}, f32[512,2,256]{2,0,1:T(8,128)}, u32[]{:S(2)}) copy-start(f32[512,2,256]{2,0,1:T(8,128)} %convolution_bitcast_fusion.8) | copy-start | bytes 3145732
  208.8 3.5 %copy-start = (f32[256,2,1024]{2,0,1:T(8,128)S(1)}, f32[256,2,1024]{2,0,1:T(8,128)}, u32[]{:S(2)}) copy-start(f32[256,2,1024]{2,0,1:T(8,128)} %convolution_bitcast_fusion.3) | copy-start | bytes 6291460
  208.8 3.5 %copy-start.3 = (f32[512,2,256]{2,0,1:T(8,128)S(1)}, f32[512,2,256]{2,0,1:T(8,128)}, u32[]{:S(2)}) copy-start(f32[512,2,256]{2,0,1:T(8,128)} %convolution_bitcast_fusion.11) | copy-start | bytes 3145732
Sparse Core Ops, SparseCore 0:
  147.3 24.2 reduce-scatter.1
where the time goes:
time: 235 us; the launch traced here: 234 us
  blocking collectives  103 us (44%)
  between operations  41.8 us (18%)
  other arithmetic  34.3 us (15%)
  local copies, waits for them, and re-layouts  23.4 us (10%)
  matrix products  21.1 us (9%)
  waiting for transfers between devices  10.5 us (4%)
    all_to_all x1, blocking collectives, shards(): lax.all_to_all(picked, 'tp', split_axis=1, concat_axis=0, tiled=True)  100 us
    gather x2, local copies, waits for them, and re-layouts, shards(): picked = jnp.take(peram, owner_times, axis=1)  18.5 us
    reduce_scatter x1, waiting for transfers between devices, shards(): lax.psum_scatter(jnp.stack([contract_rows(factor[:, time_slot], right_pai...  10.4 us
    dot_general x2, matrix products, contract_rows(): lax.dot_general(left_rows, right_pair, (((1, 2), (2, 3)), ((), ())), pref...  9.05 us
    dot_general x8, matrix products, shards(): lax.dot_general(col_block, right_four, (((1, 2), (0, 1)), ((), ())), pref...  7.78 us
    reduce_sum x4, other arithmetic, shards(): jnp.sum(product[:, 0] * partner[:, 1] + product[:, 1] * partner[:, 0])  7.01 us
    another operation x1, other arithmetic, shards(): jnp.stack([contract_rows(factor[:, time_slot], right_pairs[time_slot]) fo...  6.57 us
  transfers between devices with their start and end apart: 1, of which 1 were waited for; matrix products, arithmetic and copies ran while one was open for 2% of the time, Pallas kernels for 0%

commit v1 on v0

--- a/solution.py
+++ b/solution.py
@@ -1,7 +1,19 @@
+import functools
 import jax
 import jax.numpy as jnp
 from jax import lax
 from jax.sharding import PartitionSpec as P
+
+
+def assign_samples(state, device_axis):
+    f_now = jax.lax.all_to_all(
+        jnp.stack(jnp.split(state, jax.lax.axis_size(device_axis), 1)), device_axis, 0, 0
+    )
+    fresh = jnp.concatenate(f_now, 0)
+    return fresh
+
+
+digits_divide = functools.partial(assign_samples, device_axis="tp")
 
 
 def paired_rhs(factor_part):
@@ -27,7 +39,7 @@
     rb_count = lax.axis_size("rb")
     rb_rank = lax.axis_index("rb")
     picked = jnp.take(peram, owner_times, axis=1)
-    arrived = lax.all_to_all(picked, "tp", split_axis=1, concat_axis=0, tiled=True)
+    arrived = digits_divide(picked)
     factor = arrived[:, 0]
     total_rows = factor.shape[0]
     row_count = total_rows // rb_count

time: 235 us -> 244 us (1.038)
  matrix products: 21.1 us -> 27.7 us
    dot_general x8, matrix products: 7.78 us -> 11.8 us  [shards(): lax.dot_general(col_block, right_four, (((1, 2), (0, 1)), ((), ())), pref...]
    reduce_sum x4, other arithmetic: 7.01 us -> 10.3 us  [shards(): jnp.sum(product[:, 0] * partner[:, 1] + product[:, 1] * partner[:, 0])]
    dot_general x4, matrix products: 4.22 us -> 6.85 us  [shards(): lax.dot_general(left_three, meson_a[spin_local * eig_count:(spin_local +...]
where the time goes in v1:
time: 244 us; the launch traced here: 243 us
  blocking collectives  103 us (42%)
  between operations  42.5 us (17%)
  other arithmetic  34.7 us (14%)
  matrix products  27.7 us (11%)
  local copies, waits for them, and re-layouts  24.6 us (10%)
  waiting for transfers between devices  10.5 us (4%)
    all_to_all x1, blocking collectives, assign_samples(): jax.lax.all_to_all(jnp.stack(jnp.split(state, jax.lax.axis_size(device_ax...  100 us
    gather x2, local copies, waits for them, and re-layouts, shards(): picked = jnp.take(peram, owner_times, axis=1)  18.5 us
    dot_general x8, matrix products, shards(): lax.dot_general(col_block, right_four, (((1, 2), (0, 1)), ((), ())), pref...  11.8 us
    reduce_scatter x1, waiting for transfers between devices, shards(): lax.psum_scatter(jnp.stack([contract_rows(factor[:, time_slot], right_pai...  10.5 us
    reduce_sum x4, other arithmetic, shards(): jnp.sum(product[:, 0] * partner[:, 1] + product[:, 1] * partner[:, 0])  10.3 us
    dot_general x2, matrix products, contract_rows(): lax.dot_general(left_rows, right_pair, (((1, 2), (2, 3)), ((), ())), pref...  9.05 us
    dot_general x4, matrix products, shards(): lax.dot_general(left_three, meson_a[spin_local * eig_count:(spin_local +...  6.85 us
    another operation x1, other arithmetic, shards(): jnp.stack([contract_rows(factor[:, time_slot], right_pairs[time_slot]) fo...  6.57 us
  transfers between devices with their start and end apart: 1, of which 1 were waited for; matrix products, arithmetic and copies ran while one was open for 2% of the time, Pallas kernels for 0%

profile of v1, /device:TPU:0, one launch (start us, length us, event | category | flops | bytes accessed | tf_op | source)
XLA Modules:
  0.0 242.7 jit_solution(16414325433598682648)
XLA Ops:
  6.5 0.7 compare_select_fusion
  7.2 0.7 compare_and_fusion
  8.1 13.4 %gather_fusion = bf16[16,128,2,512]{3,2,1,0:T(2,128)(2,1)} fusion(bf16[128,24,2,512]{3,2,1,0:T(2,128)(2,1)} %param.5, s32[1024]{0:T(1024)S(1)} %pad_clamp_fusion), kind=kCustom, calls=%fused_computation | custom fusion | bytes 8388672 | tf_op jit(solution)/shard_map/jit(_take)/gather | solution.py:41
  21.5 5.1 %copy.54 = bf16[16,128,2,512]{3,1,2,0:T(8,128)(2,1)} copy(bf16[16,128,2,512]{3,2,1,0:T(2,128)(2,1)} %gather_fusion) | data formatting | bytes 8388608 | tf_op jit(solution)/shard_map/jit(_take)/gather | solution.py:41
  26.7 2.6 %select_bitcast_fusion = bf16[128,8,2,2,512]{4,0,3,2,1:T(8,128)(2,1)S(1)} fusion(bf16[8,2,128,2,512]{4,2,3,1,0:T(8,128)(2,1)} %bitcast.413, pred[8,2]{1,0:T(8,128)(4,1)S(1)} %copy.52), kind=kLoop, calls=%fused_computation.38 | loop fusion | flops 2097152 | bytes 8388624 | tf_op jit(solution)/shard_map/jit(_take)/select_n | solution.py:41
  29.7 100.3 %all_to_all.5 = bf16[8,128,1,2,2,512]{5,1,4,3,2,0:T(8,128)(2,1)S(1)} all-to-all(bf16[8,128,1,2,2,512]{5,1,4,3,2,0:T(8,128)(2,1)S(1)} %fusion.36), channel_id=1, replica_groups=mesh['grp'=2,'tp'=8,'rb'=2] {'tp'}, dimensions={0} | all-to-all | bytes 8388608 | tf_op jit(solution)/shard_map/all_to_all | solution.py:9
  130.0 0.4 copy.55
  130.4 0.7 slice_bitcast_fusion.3
  131.2 0.3 fusion.60
  131.4 0.2 maximum_bitcast_fusion
  131.6 4.5 %fusion.11 = f32[1024,1,2,1024]{3,0,2,1:T(8,128)S(1)} fusion(bf16[1,1024,2,512]{3,1,2,0:T(8,128)(2,1)S(1)} %maximum_bitcast_fusion, bf16[1,1024,2,512]{3,1,2,0:T(8,128)(2,1)S(1)} %get-tuple-element.61, bf16[1024,2,2,512]{3,0,2,1:T(8,128)(2,1)S(1)} %bitcast.411), kind=kOutput, calls=%fused_computation.40 | convolution fusion | flops 4303355904 | bytes 14680064 | tf_op jit(solution)/shard_map/dot_general | solution.py:25
  136.2 0.2 maximum_bitcast_fusion.1
  136.4 4.5 %fusion.8 = f32[1024,1,2,1024]{3,0,2,1:T(8,128)S(1)} fusion(bf16[1,1024,2,512]{3,1,2,0:T(8,128)(2,1)S(1)} %maximum_bitcast_fusion.1, bf16[1,1024,2,512]{3,1,2,0:T(8,128)(2,1)S(1)} %get-tuple-element.62, bf16[1024,2,2,512]{3,0,2,1:T(8,128)(2,1)S(1)} %bitcast.412), kind=kOutput, calls=%fused_computation.39 | convolution fusion | flops 4303355904 | bytes 14680064 | tf_op jit(solution)/shard_map/dot_general | solution.py:25
  140.9 6.6 %pad_maximum_fusion = f32[1024,2,2,1024]{3,0,2,1:T(8,128)} fusion(f32[1024,1,2,1024]{3,0,2,1:T(8,128)S(1)} %fusion.8, f32[1024,1,2,1024]{3,0,2,1:T(8,128)S(1)} %fusion.11), kind=kLoop, calls=%fused_computation.1 | loop fusion | flops 4194304 | bytes 33554432 | tf_op jit(solution)/shard_map/stack | solution.py:52
  147.5 0.6 copy-done.14
  148.2 0.6 fusion.62
  157.5 0.8 maximum_bitcast_fusion.2
  158.4 0.8 maximum_bitcast_fusion.6
  159.4 1.1 convert_bitcast_fusion
  160.5 0.9 bitcast_convert_fusion.4
  161.4 10.5 %reduce-scatter.2.cloned.1.call-done = f32[512,2,2,1024]{3,0,2,1:T(8,128)} async-done(((f32[1024,2,2,1024]{3,0,2,1:T(8,128)}), f32[512,2,2,1024]{3,0,2,1:T(8,128)}) %reduce-scatter.2.cloned.1.call-update) | async-done | bytes 8388624 | tf_op jit(solution)/shard_map/reduce_scatter | solution.py:51
  171.9 4.0 %convert_element_type.59 = bf16[512,2,2,1024]{3,0,2,1:T(8,128)(2,1)S(1)} convert(f32[512,2,2,1024]{3,0,2,1:T(8,128)} %reduce-scatter.2.cloned.1.call-done) | non-fusion elementwise | flops 2097152 | bytes 12582912 | tf_op jit(solution)/shard_map/convert_element_type | solution.py:60
  175.9 0.4 fusion.59
  176.4 0.2 slice_bitcast_fusion
  176.6 0.8 copy-done.11
  177.3 1.4 convolution_bitcast_fusion.10
  178.8 1.5 convolution_bitcast_fusion.9
  180.2 2.0 convolution_bitcast_fusion.2
  182.3 2.0 convolution_bitcast_fusion.3
  184.3 1.5 convolution_bitcast_fusion.11
  185.8 1.5 convolution_bitcast_fusion.8
  187.3 1.5 convolution_bitcast_fusion.7
  188.7 1.5 convolution_bitcast_fusion.4
  190.2 1.5 convolution_bitcast_fusion.6
  191.8 0.7 convolution_bitcast_fusion.1
  192.5 2.1 convolution_bitcast_fusion
  194.6 1.4 convolution_bitcast_fusion.5
  196.1 0.9 bitcast_convert_fusion.2
  197.0 0.9 bitcast_convert_fusion.3
  197.8 1.1 add_reduce_fusion.12
  201.6 2.2 add_reduce_fusion.14
  206.3 4.3 %add_reduce_fusion.5 = (f32[]{:T(128)}, f32[]{:T(128)}, f32[]{:T(128)}, f32[]{:T(128)}, f32[512,1,256]{2,0,1:T(8,128)S(1)}) fusion(f32[512,2,256]{2,0,1:T(8,128)} %convolution_bitcast_fusion.9, f32[256,2,1024]{2,0,1:T(8,128)} %convolution_bitcast_fusion.2, f32[256,2,1024]{2,0,1:T(8,128)} %convolution_bitcast_fusion.3, ...), kind=kLoop, calls=%fused_computation.121 | loop fusion | flops 3276796 | bytes 6815760 | tf_op jit(solution)/shard_map/reduce_sum | solution.py:114
  210.6 0.2 copy-done.9
  210.8 1.2 add_reduce_fusion.4
  222.4 3.5 %add_reduce_fusion.1 = (f32[]{:T(128)}, f32[]{:T(128)}, f32[]{:T(128)}, f32[]{:T(128)}, f32[512,1,256]{2,0,1:T(8,128)S(1)}) fusion(f32[512,2,256]{2,0,1:T(8,128)} %convolution_bitcast_fusion.5, f32[256,2,1024]{2,0,1:T(8,128)} %convolution_bitcast_fusion, f32[256,2,1024]{2,0,1:T(8,128)S(1)} %convolution_bitcast_fusion.1, ...), kind=kLoop, calls=%fused_computation.113 | loop fusion | flops 3276796 | bytes 6815760 | tf_op jit(solution)/shard_map/reduce_sum | solution.py:114
  225.9 1.3 add_reduce_fusion
  232.6 2.5 %all-reduce = (f32[1,6]{1,0:T(1,128)S(1)}, f32[1,6]{1,0:T(1,128)S(1)}) all-reduce(f32[1,6]{1,0:T(1,128)S(1)} %bitcast.419, f32[1,6]{1,0:T(1,128)S(1)} %bitcast.418), channel_id=1, replica_groups=mesh['grp'=2,'tp'=8,'rb'=2] {'rb'}, use_global_device_ids=true, to_apply=%region_34.35 | all-reduce | flops 12 | bytes 96 | tf_op jit(solution)/shard_map/psum | solution.py:142
  235.3 0.6 copy.68
  (66 shorter events, 1.9 us)
Async XLA Ops:
  6.5 165.3 %reduce-scatter.2.cloned.1.call-start = ((), (), s32[]{:S(2)}) async-start(), calls=%async_computation.2 | async-start | bytes 25165824 | tf_op jit(solution)/shard_map/reduce_scatter | solution.py:51
  147.5 0.7 copy-start.14
  147.5 8.7 %copy-start.10 = (bf16[7,2,256,256]{3,2,1,0:T(8,128)(2,1)S(1)}, bf16[7,2,256,256]{3,2,1,0:T(8,128)(2,1)}, u32[]{:S(2)}) copy-start(bf16[7,2,256,256]{3,2,1,0:T(8,128)(2,1)} %param.6) | copy-start | bytes 5505028
  176.4 1.0 copy-start.11
  182.3 5.0 %copy-start.12 = (bf16[1,256,2,256]{1,3,2,0:T(8,128)(2,1)S(1)}, bf16[1,256,2,256]{1,3,2,0:T(8,128)(2,1)}, u32[]{:S(2)}) copy-start(bf16[1,256,2,256]{1,3,2,0:T(8,128)(2,1)} %get-tuple-element.93) | copy-start | bytes 786436
  182.3 5.0 %copy-start.13 = (bf16[1,256,2,256]{1,3,2,0:T(8,128)(2,1)S(1)}, bf16[1,256,2,256]{1,3,2,0:T(8,128)(2,1)}, u32[]{:S(2)}) copy-start(bf16[1,256,2,256]{1,3,2,0:T(8,128)(2,1)} %get-tuple-element.94) | copy-start | bytes 786436
  192.5 5.3 %copy-start.4 = (f32[2,256,256]{2,1,0:T(8,128)S(1)}, f32[2,256,256]{2,1,0:T(8,128)}, u32[]{:S(2)}) copy-start(f32[2,256,256]{2,1,0:T(8,128)} %get-tuple-element.107) | copy-start | bytes 1572868
  192.5 5.3 %copy-start.5 = (f32[2,256,256]{2,1,0:T(8,128)S(1)}, f32[2,256,256]{2,1,0:T(8,128)}, u32[]{:S(2)}) copy-start(f32[2,256,256]{2,1,0:T(8,128)} %get-tuple-element.108) | copy-start | bytes 1572868
  194.6 7.0 %copy-start.3 = (f32[2,256,256]{2,1,0:T(8,128)S(1)}, f32[2,256,256]{2,1,0:T(8,128)}, u32[]{:S(2)}) copy-start(f32[2,256,256]{2,1,0:T(8,128)} %get-tuple-element.106) | copy-start | bytes 1572868
  203.7 6.9 %copy-start.8 = (f32[512,2,256]{2,0,1:T(8,128)S(1)}, f32[512,2,256]{2,0,1:T(8,128)}, u32[]{:S(2)}) copy-start(f32[512,2,256]{2,0,1:T(8,128)} %convolution_bitcast_fusion.11) | copy-start | bytes 3145732
  206.3 4.3 %copy-start.1 = (f32[256,2,1024]{2,0,1:T(8,128)S(1)}, f32[256,2,1024]{2,0,1:T(8,128)}, u32[]{:S(2)}) copy-start(f32[256,2,1024]{2,0,1:T(8,128)} %convolution_bitcast_fusion.2) | copy-start | bytes 6291460
  206.3 4.3 %copy-start.2 = (f32[256,2,1024]{2,0,1:T(8,128)S(1)}, f32[256,2,1024]{2,0,1:T(8,128)}, u32[]{:S(2)}) copy-start(f32[256,2,1024]{2,0,1:T(8,128)} %convolution_bitcast_fusion.3) | copy-start | bytes 6291460
  206.3 4.5 %copy-start.9 = (f32[512,2,256]{2,0,1:T(8,128)S(1)}, f32[512,2,256]{2,0,1:T(8,128)}, u32[]{:S(2)}) copy-start(f32[512,2,256]{2,0,1:T(8,128)} %convolution_bitcast_fusion.8) | copy-start | bytes 3145732
  212.1 13.8 %copy-start.6 = (f32[512,2,256]{2,0,1:T(8,128)S(1)}, f32[512,2,256]{2,0,1:T(8,128)}, u32[]{:S(2)}) copy-start(f32[512,2,256]{2,0,1:T(8,128)} %convolution_bitcast_fusion.7) | copy-start | bytes 3145732
  222.4 3.5 %copy-start = (f32[256,2,1024]{2,0,1:T(8,128)S(1)}, f32[256,2,1024]{2,0,1:T(8,128)}, u32[]{:S(2)}) copy-start(f32[256,2,1024]{2,0,1:T(8,128)} %convolution_bitcast_fusion) | copy-start | bytes 6291460
  222.4 3.5 %copy-start.7 = (f32[512,2,256]{2,0,1:T(8,128)S(1)}, f32[512,2,256]{2,0,1:T(8,128)}, u32[]{:S(2)}) copy-start(f32[512,2,256]{2,0,1:T(8,128)} %convolution_bitcast_fusion.4) | copy-start | bytes 3145732
Sparse Core Ops, SparseCore 0:
  147.6 24.2 reduce-scatter.1
